TPU v7x, 32 devices: a whole 2x2x4 slice. The times are simulated.
32 devices in a mesh: groups: 2 (over y), seq: 4 (over z), head: 4 (over x, core).
Axes of the slice: x: 2, y: 2, z: 4, core: 2. Of those that a mesh axis runs over, the one named last changes fastest.
Arguments:
- query_latent_rows: bfloat16 [640, 1536], P(('groups', 'seq')), parts along dimension 0, may hold values from -6 to 6
- key_value_latents: bfloat16 [640, 576], P(('groups', 'seq')), parts along dimension 0, may hold values from -500 to 500
- positions: int32 [640], P(('groups', 'seq')), parts along dimension 0, may hold values from 130752 to 131071, as said below
- query_up_weight: bfloat16 [1536, 12288], P('seq', 'head'), may hold values from -0.15625 to 0.15625
- adapter_down_factor: bfloat16 [3072, 64], P(('groups', 'seq')), parts along dimension 0, may hold values from -0.75 to 0.75
- adapter_up_factor: bfloat16 [128, 12288], P('groups', 'head'), parts along dimension 0, may hold values from -0.15625 to 0.15625
- head_key_up_weight: bfloat16 [64, 128, 512], P('head'), may hold values from -0.5 to 0.5
- head_value_up_weight: bfloat16 [64, 512, 128], P('head'), may hold values from -0.25 to 0.25
- output_projection_weight: bfloat16 [8192, 7168], P('head', 'seq'), may hold values from -0.0625 to 0.0625
Outputs:
- merged_weight: bfloat16 [3072, 12288], P(('groups', 'seq'), 'head'), parts along dimension 0
- mixed: bfloat16 [640, 7168], P(('groups', 'head'), 'seq'), parts along dimension 0
There are 2 independent parts, one for each index of `groups`. A program takes and returns all parts, laid end to end along the dimension named above; an argument that names none is the same for every part. Nothing has to cross between parts.
Inputs may be any that keep to these rules, and one draw needn't show every extreme that they name: positions are distinct; each aligned block of 80 rows holds 80 consecutive positions in rising order, and the blocks together cover the last 320 positions of the prompt in an order drawn from the seed.
All inputs are finite; a program needn't handle non-finite values.
Results may differ from a plain program's by a relative error of at most 0.015.
The roundings to bfloat16 on the way count: a program that leaves them out, or rounds other values in their place, can miss the bound.
Values may be sent and summed in bfloat16 or wider, within the bound.
A program may use at most 64 MiB of HBM per device.

v0:
```python
import math

import jax
import jax.numpy as jnp
from jax import lax
from jax.sharding import PartitionSpec as P


def on_device(
    query_latent_rows,
    key_value_latents,
    positions,
    query_up_weight,
    adapter_down_factor,
    adapter_up_factor,
    head_key_up_weight,
    head_value_up_weight,
    output_projection_weight,
):
    merged_query_weight = (
        query_up_weight.astype(jnp.float32)
        + jnp.dot(adapter_down_factor, adapter_up_factor, preferred_element_type=jnp.float32)
    ).astype(jnp.bfloat16)
    tok_rows = query_latent_rows.shape[0]
    queries = jnp.dot(
        query_latent_rows,
        lax.all_gather(merged_query_weight, "seq", axis=0, tiled=True),
        preferred_element_type=jnp.float32,
    )
    heads_dev = head_key_up_weight.shape[0]
    nope_dim = head_key_up_weight.shape[1]
    kv_rank = head_key_up_weight.shape[2]
    lat_width = key_value_latents.shape[1]
    score_scale = 1.0 / math.sqrt(nope_dim + lat_width - kv_rank)
    queries = queries.astype(jnp.bfloat16).reshape(tok_rows, heads_dev, -1)
    absorbed = jnp.einsum(
        "thn,hnk->thk",
        queries[:, :, :nope_dim],
        head_key_up_weight,
        preferred_element_type=jnp.float32,
    ).astype(jnp.bfloat16)
    full_query = jnp.concatenate([absorbed, queries[:, :, nope_dim:]], axis=2).reshape(
        tok_rows * heads_dev, lat_width
    )
    query_pos = jnp.repeat(positions, heads_dev)
    q_count = tok_rows * heads_dev
    row_max = jnp.full((q_count,), -1e30, jnp.float32)
    key_rows = lax.all_gather(key_value_latents, "seq", axis=0, tiled=True)
    key_pos = lax.all_gather(positions, "seq", axis=0, tiled=True)
    visible = key_pos[None, :] <= query_pos[:, None]
    scores = (
        lax.dot_general(
            full_query, key_rows, (((1,), (1,)), ((), ())), preferred_element_type=jnp.float32
        )
        * score_scale
    )
    scores = jnp.where(visible, scores, jnp.float32(-1e30))
    new_max = jnp.maximum(row_max, jnp.max(scores, axis=1))
    weights = jnp.where(visible, jnp.exp(scores - new_max[:, None]), jnp.float32(0.0))
    row_sum = jnp.sum(weights, axis=1)
    running = jnp.dot(
        weights.astype(jnp.bfloat16), key_rows[:, :kv_rank], preferred_element_type=jnp.float32
    )
    row_max, row_sum, running = (new_max, row_sum, running)
    context_output = (
        (running / row_sum[:, None]).astype(jnp.bfloat16).reshape(tok_rows, heads_dev, kv_rank)
    )
    heads_out = (
        jnp.einsum(
            "euw,uwz->euz", context_output, head_value_up_weight, preferred_element_type=jnp.float32
        )
        .astype(jnp.bfloat16)
        .reshape(tok_rows, -1)
    )
    partial_value = jnp.dot(
        lax.all_gather(heads_out, "seq", axis=0, tiled=True),
        output_projection_weight,
        preferred_element_type=jnp.float32,
    )
    mixed = lax.psum_scatter(
        partial_value.astype(jnp.bfloat16), "head", scatter_dimension=0, tiled=True
    )
    return (merged_query_weight, mixed)


def solution(mesh):
    placed = (
        P(("groups", "seq"), None),
        P(("groups", "seq"), None),
        P(("groups", "seq")),
        P("seq", "head"),
        P(("groups", "seq"), None),
        P("groups", "head"),
        P("head", None, None),
        P("head", None, None),
        P("head", "seq"),
    )
    return jax.shard_map(
        on_device,
        mesh=mesh,
        in_specs=placed,
        out_specs=(P(("groups", "seq"), "head"), P(("groups", "head"), "seq")),
        check_vma=False,
    )
```

profile of v0, /device:TPU:0, one launch (start us, length us, event | category | flops | bytes accessed | tf_op | source)
XLA Modules:
  0.0 269.0 jit_solution(17031424686050613375)
XLA Ops:
  7.2 0.0 copy-start
  7.2 0.0 all-gather.3.cloned.1.call-start
  7.2 4.2 %add_convert_fusion = bf16[384,3072]{1,0:T(8,128)(2,1)} fusion(bf16[384,3072]{1,0:T(8,128)(2,1)} %param.12, bf16[384,64]{0,1:T(8,128)(2,1)} %param.13, bf16[64,3072]{1,0:T(8,128)(2,1)} %param.14), kind=kOutput, calls=%fused_computation | convolution fusion | flops 154533888 | bytes 5160960 | tf_op jit(solution)/shard_map/dot_general | solution.py:22
  11.4 0.0 copy-start.5
  11.4 0.0 copy-start.6
  11.4 0.0 copy-start.4
  11.4 0.0 copy-start.2
  11.4 0.0 all-gather.3.cloned.1.call-update
  11.4 0.0 all-gather.5.cloned.1.call-start
  11.5 0.6 copy-done.5
  12.0 0.1 broadcast_in_dim.16
  12.1 0.1 le.16
  12.2 0.0 copy-done.6
  12.2 0.6 dynamic-slice
  13.4 0.2 dynamic-update-slice
  13.7 9.9 %all-reduce = s32[320]{0:T(512)S(1)} all-reduce(s32[320]{0:T(512)S(1)} %dynamic-update-slice), channel_id=1, replica_groups=mesh['groups'=2,'seq'=4,'head'=4] {'seq'}, use_global_device_ids=true, to_apply=%add | all-reduce | flops 320 | bytes 2560
  23.6 0.0 copy-done.4
  23.6 25.1 %all_gather.14 = bf16[320,576]{1,0:T(8,128)(2,1)} all-gather(bf16[80,576]{1,0:T(8,128)(2,1)S(1)} %copy-done.4), channel_id=1, replica_groups=mesh['groups'=2,'seq'=4,'head'=4] {'seq'}, dimensions={0}, use_global_device_ids=true | all-gather | bytes 460800 | tf_op jit(solution)/shard_map/all_gather | solution.py:48
  48.7 137.6 %all-gather.3.cloned.1.call-done = bf16[1536,3072]{1,0:T(8,128)(2,1)} async-done(((bf16[384,3072]{1,0:T(8,128)(2,1)}), bf16[1536,3072]{1,0:T(8,128)(2,1)}) %all-gather.3.cloned.1.call-update) | async-done | bytes 9437200 | tf_op jit(solution)/shard_map/all_gather | solution.py:27
  186.3 0.0 copy-done.2
  186.3 5.4 %fusion = bf16[80,3072]{1,0:T(8,128)(2,1)S(1)} fusion(bf16[80,1536]{1,0:T(8,128)(2,1)S(1)} %copy-done.2, bf16[1536,3072]{1,0:T(8,128)(2,1)} %all-gather.3.cloned.1.call-done), kind=kOutput, calls=%fused_computation.2 | convolution fusion | flops 755220480 | bytes 10174464 | tf_op jit(solution)/shard_map/dot_general | solution.py:25
  191.8 0.7 reshape.22
  192.5 0.1 slice.12
  192.6 0.1 slice.13
  192.6 0.1 copy.20
  192.7 0.0 copy-done
  192.7 0.5 fusion.3
  193.2 0.1 pad_maximum_fusion
  193.4 0.0 copy-start.3
  193.4 0.3 copy.16
  193.7 0.7 copy-done.3
  194.4 0.9 fusion.22
  195.3 0.3 fusion.6
  195.6 0.0 copy-start.1
  195.6 1.0 fusion.1
  196.6 0.6 copy-done.1
  197.2 1.6 fusion.11
  198.8 0.8 copy.31
  199.6 0.0 all-gather.5.cloned.1.call-update
  199.7 0.0 reduce-scatter.2.cloned.1.call-start
  199.7 31.0 %all-gather.5.cloned.1.call-done = bf16[320,2048]{1,0:T(8,128)(2,1)} async-done(((bf16[80,2048]{1,0:T(8,128)(2,1)}), bf16[320,2048]{1,0:T(8,128)(2,1)}) %all-gather.5.cloned.1.call-update) | async-done | bytes 1310736 | tf_op jit(solution)/shard_map/all_gather | solution.py:76
  230.7 7.0 %convolution_convert_fusion.1 = bf16[320,1792]{1,0:T(8,128)(2,1)} fusion(bf16[320,2048]{1,0:T(8,128)(2,1)} %all-gather.5.cloned.1.call-done, bf16[2048,1792]{1,0:T(8,128)(2,1)} %param.17), kind=kOutput, calls=%fused_computation.7 | convolution fusion | flops 2349383680 | bytes 9797632 | tf_op jit(solution)/shard_map/dot_general | solution.py:75
  237.7 0.0 reduce-scatter.2.cloned.1.call-update
  237.8 24.7 %reduce-scatter.2.cloned.1.call-done = bf16[80,1792]{1,0:T(8,128)(2,1)} async-done(((bf16[320,1792]{1,0:T(8,128)(2,1)}), bf16[80,1792]{1,0:T(8,128)(2,1)}) %reduce-scatter.2.cloned.1.call-update) | async-done | bytes 286736 | tf_op jit(solution)/shard_map/reduce_scatter | solution.py:80
  (2 shorter events, 0.0 us)
Async XLA Ops:
  7.2 185.6 %copy-start = (bf16[16,128,512]{2,1,0:T(8,128)(2,1)S(1)}, bf16[16,128,512]{2,1,0:T(8,128)(2,1)}, u32[]{:S(2)}) copy-start(bf16[16,128,512]{2,1,0:T(8,128)(2,1)} %param.15) | copy-start | bytes 6291460
  7.2 179.2 %all-gather.3.cloned.1.call-start = ((), (), s32[]{:S(2)}) async-start(), calls=%async_computation.1 | async-start | bytes 11796480 | tf_op jit(solution)/shard_map/all_gather | solution.py:27
  11.4 0.7 copy-start.5
  11.4 0.8 copy-start.6
  11.4 12.2 %copy-start.4 = (bf16[80,576]{1,0:T(8,128)(2,1)S(1)}, bf16[80,576]{1,0:T(8,128)(2,1)}, u32[]{:S(2)}) copy-start(bf16[80,576]{1,0:T(8,128)(2,1)} %param.10) | copy-start | bytes 276484
  11.4 175.0 %copy-start.2 = (bf16[80,1536]{1,0:T(8,128)(2,1)S(1)}, bf16[80,1536]{1,0:T(8,128)(2,1)}, u32[]{:S(2)}) copy-start(bf16[80,1536]{1,0:T(8,128)(2,1)} %param.9) | copy-start | bytes 737284
  11.4 219.3 %all-gather.5.cloned.1.call-start = ((), (), s32[]{:S(2)}) async-start(), calls=%async_computation.2 | async-start | bytes 1638400 | tf_op jit(solution)/shard_map/all_gather | solution.py:76
  193.4 1.0 copy-start.3
  195.6 1.6 copy-start.1
  199.7 62.8 %reduce-scatter.2.cloned.1.call-start = ((), (), s32[]{:S(2)}) async-start(), calls=%async_computation.3 | async-start | bytes 1433600 | tf_op jit(solution)/shard_map/reduce_scatter | solution.py:80
Sparse Core Ops, SparseCore 0:
  11.5 174.7 all-gather.2
  199.8 30.8 all-gather.4
  237.9 24.5 reduce-scatter.1
where the time goes:
time: 269 us
  waiting for transfers between devices  193 us (72%)
  blocking collectives  35 us (13%)
  matrix products  20.6 us (8%)
  between operations  14.5 us (5%)
  local copies, waits for them, and re-layouts  4.87 us (2%)
    all_gather x1, waiting for transfers between devices, on_device(): lax.all_gather(merged_query_weight, 'seq', axis=0, tiled=True)  138 us
    all_gather x1, waiting for transfers between devices, on_device(): lax.all_gather(heads_out, 'seq', axis=0, tiled=True)  31 us
    all_gather x1, blocking collectives, on_device(): key_rows = lax.all_gather(key_value_latents, 'seq', axis=0, tiled=True)  25.1 us
    reduce_scatter x1, waiting for transfers between devices, on_device(): lax.psum_scatter(partial_value.astype(jnp.bfloat16), 'head', scatter_dime...  24.7 us
    unnamed x1, blocking collectives  9.92 us
    dot_general x1, matrix products, on_device(): jnp.dot(lax.all_gather(heads_out, 'seq', axis=0, tiled=True), output_proj...  7.02 us
    dot_general x1, matrix products, on_device(): jnp.dot(query_latent_rows, lax.all_gather(merged_query_weight, 'seq', axi...  5.42 us
  transfers between devices with their start and end apart: 3, of which 3 were waited for; matrix products, arithmetic and copies ran while one was open for 0% of the time, Pallas kernels for 0%

commit v1 on v0

--- a/solution.py
+++ b/solution.py
@@ -1,9 +1,260 @@
+import functools
 import math
 
 import jax
 import jax.numpy as jnp
 from jax import lax
+from jax.experimental import pallas as pl
+from jax.experimental.pallas import tpu as pltpu
 from jax.sharding import PartitionSpec as P
+
+
+MESH = pl.DeviceIdType.MESH
+
+
+def fused_kernel(dims, w, xk, a, pos, b, key_up, value_up, out_proj, merged, mixed,
+                 w_v, a_v, b_v, m_v, xk_all, a_all, pos_all, w_all, mm, ku_v, vu_v, op_v, heads, total,
+                 part, got, loc, sx, rx, sy, ry, sa, ra, sb, rb, sp, rp, sw, rw, sv, rv, sh, rh, so, ro):
+    S, H, C, T, KQ, NC, nope, rope, kvr, hp, cw, dcols, scale = dims
+    qw = nope + rope
+    half_k = KQ // 2
+    half_x = xk.shape[1] // 2
+    ql = S * KQ
+    pw = (cw // qw) * (out_proj.shape[0] // (hp * S))
+    heads_c = cw // qw
+    vdim = out_proj.shape[0] // (hp * S)
+    s = lax.axis_index("seq")
+    g = lax.axis_index("groups")
+    h = lax.axis_index("head")
+    other = 1 - g
+    core = lax.rem(h, 2)
+    sibling = h + 1 - 2 * core
+
+    barrier = pltpu.get_barrier_semaphore()
+    for k in range(1, S):
+        pl.semaphore_signal(barrier, inc=1, device_id={"seq": lax.rem(s + k, S)}, device_id_type=MESH)
+    for k in range(1, H):
+        pl.semaphore_signal(barrier, inc=1, device_id={"head": lax.rem(h + k, H)}, device_id_type=MESH)
+    pl.semaphore_signal(barrier, inc=1, device_id={"groups": other}, device_id_type=MESH)
+    pl.semaphore_wait(barrier, S + H - 1)
+
+    def remote(src, dst, ss, rs, **dev):
+        return pltpu.make_async_remote_copy(
+            src_ref=src, dst_ref=dst, send_sem=ss, recv_sem=rs, device_id=dev, device_id_type=MESH)
+
+    sends = []
+
+    def go(c):
+        c.start()
+        sends.append(c)
+        return c
+
+    def rows(i):
+        return pl.ds(pl.multiple_of(i * T, T), T)
+
+    def xcols(i):
+        return pl.ds(pl.multiple_of(i * half_x, 128), half_x)
+
+    def krows(i):
+        return pl.ds(pl.multiple_of(i * half_k, 16), half_k)
+
+    gx, ga, gp = {}, {}, {}
+    for k in range(1, S):
+        p = lax.rem(s + k, S)
+        gp[k] = go(remote(pos, pos_all.at[s], sp.at[k], rp.at[k], seq=p))
+        ga[k] = go(remote(a.at[krows(core)], a_all.at[s, krows(core)], sa.at[k], ra.at[k], seq=p))
+        gx[k] = go(remote(xk.at[:, xcols(core)], xk_all.at[rows(s), xcols(core)], sx.at[k], rx.at[k], seq=p))
+    gw = {}
+
+    def wcols(p, c):
+        return pl.ds(pl.multiple_of(p * (cw * C) + c * cw, 128), cw)
+
+    for c in range(C):
+        for k in range(1, S):
+            p = lax.rem(s + k, S)
+            gw[c, k] = go(remote(
+                w.at[krows(g), wcols(p, c)], w_all.at[c, s, krows(g)], sw.at[c, k], rw.at[c, k], seq=p))
+    local = []
+
+    def fetch(src, dst):
+        cp = pltpu.make_async_copy(src, dst, loc.at[len(local)])
+        cp.start()
+        local.append(cp)
+        return cp
+
+    first = [fetch(w, w_v), fetch(a, a_v), fetch(b, b_v)]
+    own = [fetch(xk, xk_all.at[rows(s)]), fetch(a, a_all.at[s]), fetch(pos, pos_all.at[s])]
+    own += [fetch(w.at[:, wcols(s, c)], w_all.at[c, s]) for c in range(C)]
+    wts = [fetch(key_up.at[pl.ds(s * hp, hp)], ku_v), fetch(value_up.at[pl.ds(s * hp, hp)], vu_v)]
+    ops = []
+    for c in range(C):
+        for i in range(S):
+            ops.append(fetch(out_proj.at[pl.ds((i * hp + c * heads_c) * vdim, pw)], op_v.at[c, pl.ds(i * pw, pw)]))
+    for cp in first:
+        cp.wait()
+
+    def merge_cols(i, carry):
+        cols = pl.ds(pl.multiple_of(i * cw, 128), cw)
+        m_v[:, cols] = (w_v[:, cols].astype(jnp.float32) + jnp.dot(
+            a_v[...], b_v[:, cols], preferred_element_type=jnp.float32)).astype(jnp.bfloat16)
+        return carry
+
+    lax.fori_loop(0, NC // cw, merge_cols, 0)
+
+    yx, ya = {}, {}
+    for k in range(1, S):
+        q = lax.rem(s - k + S, S)
+        ga[k].wait_recv()
+        ya[k] = go(remote(a_all.at[q, krows(core)], a_all.at[q, krows(core)], sb.at[k], rb.at[k], head=sibling))
+        gx[k].wait_recv()
+        yx[k] = go(remote(xk_all.at[rows(q), xcols(core)], xk_all.at[rows(q), xcols(core)], sy.at[k], ry.at[k], head=sibling))
+    out_m = pltpu.make_async_copy(m_v, merged, loc.at[len(local)])
+    out_m.start()
+
+    def forward(c):
+        res = {}
+        for k in range(1, S):
+            q = lax.rem(s - k + S, S)
+            gw[c, k].wait_recv()
+            res[k] = go(remote(w_all.at[c, q, krows(g)], w_all.at[c, q, krows(g)], sv.at[c, k], rv.at[c, k], groups=other))
+        return res
+
+    q_iota = lax.broadcasted_iota(jnp.int32, (S * T, 1), 0)
+    k_iota = lax.broadcasted_iota(jnp.int32, (1, S * T), 1)
+
+    def attend(c):
+        for i in range(S):
+            mm[i * KQ:(i + 1) * KQ] = (w_all[c, i].astype(jnp.float32) + jnp.dot(
+                a_all[i], b_v[:, wcols(s, c)], preferred_element_type=jnp.float32)).astype(jnp.bfloat16)
+        queries = jnp.dot(xk_all[:, :ql], mm[...], preferred_element_type=jnp.float32)
+        qpos = q_iota
+        kpos = k_iota
+        for i in range(S):
+            start = pos_all[i, 0:1, 0:1] - i * T
+            qpos = qpos + jnp.where(q_iota // T == i, start, 0)
+            kpos = kpos + jnp.where(k_iota // T == i, start, 0)
+        visible = kpos <= qpos
+        lat = xk_all[:, ql:ql + kvr]
+        key_rope = xk_all[:, ql + kvr:ql + kvr + rope]
+        contract = (((1,), (1,)), ((), ()))
+        for j in range(heads_c):
+            qn = queries[:, j * qw:j * qw + nope].astype(jnp.bfloat16)
+            qr = queries[:, j * qw + nope:(j + 1) * qw].astype(jnp.bfloat16)
+            absorbed = jnp.dot(qn, ku_v[c * heads_c + j], preferred_element_type=jnp.float32).astype(jnp.bfloat16)
+            scores = (lax.dot_general(absorbed, lat, contract, preferred_element_type=jnp.float32)
+                      + lax.dot_general(qr, key_rope, contract, preferred_element_type=jnp.float32)) * scale
+            scores = jnp.where(visible, scores, jnp.float32(-1e30))
+            top = jnp.max(scores, axis=1, keepdims=True)
+            weights = jnp.where(visible, jnp.exp(scores - top), jnp.float32(0.0))
+            row_sum = jnp.sum(weights, axis=1, keepdims=True)
+            context = jnp.dot(weights.astype(jnp.bfloat16), lat, preferred_element_type=jnp.float32)
+            context = (context / row_sum).astype(jnp.bfloat16)
+            res = jnp.dot(context, vu_v[c * heads_c + j], preferred_element_type=jnp.float32).astype(jnp.bfloat16)
+            heads[c, :, pl.ds(pl.multiple_of(s * pw + j * vdim, 128), vdim)] = res
+        res = {}
+        mine = pl.ds(pl.multiple_of(s * pw, 128), pw)
+        for k in range(1, S):
+            res[k] = go(remote(heads.at[c, :, mine], heads.at[c, :, mine], sh.at[c, k], rh.at[c, k], seq=lax.rem(s + k, S)))
+        return res
+
+    gh = {}
+    for c in range(C):
+        gv = forward(c)
+        if c == 0:
+            for cp in own + wts:
+                cp.wait()
+            for k in range(1, S):
+                gp[k].wait_recv()
+                ya[k].wait_recv()
+                yx[k].wait_recv()
+        for k in range(1, S):
+            gv[k].wait_recv()
+        gh[c] = attend(c)
+    for cp in ops:
+        cp.wait()
+    nb = 2
+    bw = dcols // nb
+    go_out = {}
+    for c in range(C):
+        for k in range(1, S):
+            gh[c][k].wait_recv()
+        for i in range(nb):
+            cols = slice(i * bw, (i + 1) * bw)
+            acc = jnp.dot(heads[c], op_v[c, :, cols], preferred_element_type=jnp.float32)
+            if c > 0:
+                acc = acc + total[:, cols]
+            if c < C - 1:
+                total[:, cols] = acc
+            else:
+                part[i] = acc.astype(jnp.bfloat16)
+                for k in range(1, H):
+                    p = lax.rem(h + k, H)
+                    go_out[i, k] = go(remote(
+                        part.at[i, pl.ds(pl.multiple_of(p * T, T), T)], got.at[i, k], so.at[i, k], ro.at[i, k], head=p))
+    for i in range(nb):
+        res = part[i, pl.ds(pl.multiple_of(h * T, T), T)].astype(jnp.float32)
+        for k in range(1, H):
+            go_out[i, k].wait_recv()
+            res = res + got[i, k].astype(jnp.float32)
+        mixed[:, i * bw:(i + 1) * bw] = res.astype(jnp.bfloat16)
+    for cp in sends:
+        cp.wait_send()
+    out_m.wait()
+
+
+def fused(mesh_shape, x, kv, positions, w, a, b, key_up, value_up, out_proj):
+    S, H = mesh_shape["seq"], mesh_shape["head"]
+    T, ql = x.shape
+    KQ, NC = w.shape
+    hd, nope, kvr = key_up.shape
+    rope = kv.shape[1] - kvr
+    vdim = value_up.shape[2]
+    hp = hd // S
+    heads_c = 2
+    C = hp // heads_c
+    cw = heads_c * (nope + rope)
+    dcols = out_proj.shape[1]
+    width = ql + kv.shape[1]
+    full = -(-width // 256) * 256
+    xk = jnp.concatenate([x, kv, jnp.zeros((T, full - width), x.dtype)], axis=1)
+    pos = jnp.broadcast_to(positions[:1].reshape(1, 1), (8, 128))
+    scale = 1.0 / math.sqrt(nope + rope)
+    dims = (S, H, C, T, KQ, NC, nope, rope, kvr, hp, cw, dcols, scale)
+    bf, f32 = jnp.bfloat16, jnp.float32
+    dma = pltpu.SemaphoreType.DMA
+    nloc = 3 + 3 + C + 2 + C * S + 1
+    pw = heads_c * vdim
+    return pl.pallas_call(
+        functools.partial(fused_kernel, dims),
+        out_shape=(jax.ShapeDtypeStruct((KQ, NC), bf), jax.ShapeDtypeStruct((T, dcols), bf)),
+        in_specs=[pl.BlockSpec(memory_space=pl.ANY)] * 8,
+        out_specs=(pl.BlockSpec(memory_space=pl.ANY), pl.BlockSpec(memory_space=pltpu.VMEM)),
+        scratch_shapes=[
+            pltpu.VMEM((KQ, NC), bf), pltpu.VMEM(a.shape, bf), pltpu.VMEM(b.shape, bf), pltpu.VMEM((KQ, NC), bf),
+            pltpu.VMEM((S * T, full), bf), pltpu.VMEM((S,) + a.shape, bf), pltpu.VMEM((S, 8, 128), jnp.int32),
+            pltpu.VMEM((C, S, KQ, cw), bf), pltpu.VMEM((S * KQ, cw), bf),
+            pltpu.VMEM((hp, nope, kvr), bf), pltpu.VMEM((hp, kvr, vdim), bf),
+            pltpu.VMEM((C, S * pw, dcols), bf), pltpu.VMEM((C, S * T, S * pw), bf), pltpu.VMEM((S * T, dcols), f32),
+            pltpu.VMEM((2, S * T, dcols // 2), bf), pltpu.VMEM((2, H, T, dcols // 2), bf),
+            dma((nloc,)),
+            dma((S,)), dma((S,)), dma((S,)), dma((S,)), dma((S,)), dma((S,)), dma((S,)), dma((S,)), dma((S,)), dma((S,)),
+            dma((C, S)), dma((C, S)), dma((C, S)), dma((C, S)), dma((C, S)), dma((C, S)),
+            dma((2, H)), dma((2, H)),
+        ],
+        compiler_params=pltpu.CompilerParams(collective_id=0, has_side_effects=True),
+    )(w, xk, a, pos, b, key_up, value_up, out_proj)
+
+
+def fits(shape, x, kv, w, a, key_up, value_up, out_proj):
+    S, H = shape["seq"], shape["head"]
+    hd, nope, kvr = key_up.shape
+    rope = kv.shape[1] - kvr
+    return (
+        shape["groups"] == 2 and S > 1 and H == S and H % 2 == 0 and hd % (2 * S) == 0
+        and (2 * (nope + rope)) % 128 == 0 and w.shape[0] % 32 == 0 and x.shape[0] % 16 == 0
+        and nope % 128 == 0 and kvr % 128 == 0 and value_up.shape[2] % 128 == 0
+        and x.shape[1] % 128 == 0 and out_proj.shape[1] % 256 == 0
+    )
 
 
 def on_device(
@@ -95,8 +346,14 @@
         P("head", None, None),
         P("head", "seq"),
     )
+
+    def body(x, kv, positions, w, a, b, key_up, value_up, out_proj):
+        if fits(mesh.shape, x, kv, w, a, key_up, value_up, out_proj):
+            return fused(mesh.shape, x, kv, positions, w, a, b, key_up, value_up, out_proj)
+        return on_device(x, kv, positions, w, a, b, key_up, value_up, out_proj)
+
     return jax.shard_map(
-        on_device,
+        body,
         mesh=mesh,
         in_specs=placed,
         out_specs=(P(("groups", "seq"), "head"), P(("groups", "head"), "seq")),

time: 269 us -> 103 us (0.38)
  the two profiles are of different devices: /device:TPU:0 before, /device:TPU:25 now
where the time goes in v1:
time: 103 us; the launch traced here: 102 us
  Pallas kernels  93.2 us (90%)
  local copies, waits for them, and re-layouts  8.61 us (8%)
    pallas_call x1, Pallas kernels, fused(): pl.pallas_call(functools.partial(fused_kernel, dims), out_shape=(jax.Shap...  93.2 us
    unnamed x5, local copies, waits for them, and re-layouts  5.52 us

profile of v1, /device:TPU:25, one launch (start us, length us, event | category | flops | bytes accessed | tf_op | source)
XLA Modules:
  0.0 102.4 jit_solution(5469178482973210077)
XLA Ops:
  0.6 1.2 %broadcast_in_dim.12.pos = s32[8,128]{1,0:T(8,128)} broadcast(s32[]{:T(128)} %bitcast.2), dimensions={} | broadcast | bytes 4100 | tf_op jit(solution)/shard_map/broadcast_in_dim | solution.py:220
  1.9 1.5 %copy.11.a = bf16[384,64]{1,0:T(8,128)(2,1)} copy(bf16[384,64]{0,1:T(8,128)(2,1)} %param.13) | data formatting | bytes 98304 | tf_op args[4]
  3.4 1.8 %concatenate.3.xk = bf16[80,2304]{1,0:T(8,128)(2,1)} concatenate(bf16[80,1536]{1,0:T(8,128)(2,1)} %param.9, bf16[80,576]{1,0:T(8,128)(2,1)} %param.10, bf16[80,192]{1,0:T(8,128)(2,1)S(1)} %broadcast_in_dim.10), dimensions={1} | concatenate | bytes 737280 | tf_op jit(solution)/shard_map/concatenate | solution.py:219
  5.3 93.2 %shard_map.104 = (bf16[384,3072]{1,0:T(8,128)(2,1)}, bf16[80,1792]{1,0:T(8,128)(2,1)}) custom-call(bf16[384,3072]{1,0:T(8,128)(2,1)} %w.1, bf16[80,2304]{1,0:T(8,128)(2,1)} %concatenate.3.xk, bf16[384,64]{1,0:T(8,128)(2,1)} %copy.11.a, s32[8,128]{1,0:T(8,128)} %broadcast_in_dim.12.pos, bf16[64,3072]{1,0:T(8,128)(2,1)} %b.1, bf16[16,128,512]{2,1,0:T(8,128)(2,1)} %key_up.1, ...), custom_call_target="tpu_custom_call" | custom-call | tf_op jit(solution)/shard_map/pallas_call | solution.py:227
  98.4 0.0 copy-start
  98.5 3.3 %copy.14 = bf16[384,3072]{1,0:T(8,128)(2,1)} copy(bf16[384,3072]{1,0:T(8,128)(2,1)} %get-tuple-element.4) | data formatting | bytes 4718592
  101.7 0.0 copy-done
  101.7 0.7 copy.15
  (1 shorter events, 0.0 us)
Async XLA Ops:
  98.4 3.3 %copy-start = (bf16[80,1792]{1,0:T(8,128)(2,1)S(1)}, bf16[80,1792]{1,0:T(8,128)(2,1)}, u32[]{:S(2)}) copy-start(bf16[80,1792]{1,0:T(8,128)(2,1)} %get-tuple-element.5) | copy-start | bytes 860164

commit v2 on v1

--- a/solution.py
+++ b/solution.py
@@ -12,9 +12,10 @@
 MESH = pl.DeviceIdType.MESH
 
 
-def fused_kernel(dims, w, xk, a, pos, b, key_up, value_up, out_proj, merged, mixed,
-                 w_v, a_v, b_v, m_v, xk_all, a_all, pos_all, w_all, mm, ku_v, vu_v, op_v, heads, total,
-                 part, got, loc, sx, rx, sy, ry, sa, ra, sb, rb, sp, rp, sw, rw, sv, rv, sh, rh, so, ro):
+def fused_kernel(dims, pos, w, xk, a, b, key_up, value_up, out_proj, mixed,
+                 b_v, pos_v, xk_all, a_all, pos_all, w_all, mm, ku_v, vu_v, op_v, heads, total,
+                 part, pair, mid, got, loc, sx, rx, sy, ry, sa, ra, sb, rb, sp, rp, sw, rw, sv, rv, sh, rh,
+                 st, rt, so, ro):
     S, H, C, T, KQ, NC, nope, rope, kvr, hp, cw, dcols, scale = dims
     qw = nope + rope
     half_k = KQ // 2
@@ -27,7 +28,11 @@
     g = lax.axis_index("groups")
     h = lax.axis_index("head")
     other = 1 - g
+    pos_v[...] = jnp.full(pos_v.shape, pos[0], jnp.int32)
     core = lax.rem(h, 2)
+    half_a = a.shape[0] // 2
+    X = H // 2
+    chip = h // 2
     sibling = h + 1 - 2 * core
 
     barrier = pltpu.get_barrier_semaphore()
@@ -58,22 +63,89 @@
     def krows(i):
         return pl.ds(pl.multiple_of(i * half_k, 16), half_k)
 
-    gx, ga, gp = {}, {}, {}
+    def arows(i):
+        return pl.ds(pl.multiple_of(i * half_a, 16), half_a)
+
+    class Line:
+        def __init__(self, own, place, ss, rs, hook=None):
+            self.own, self.place, self.ss, self.rs, self.hook = own, place, ss, rs, hook
+            self.open = []
+
+        def copy(self, src, q, slot, way):
+            to = lax.rem(s + way + S, S)
+            return remote(src, self.place(q), self.ss.at[slot], self.rs.at[q], seq=to)
+
+        def send(self):
+            for i, way in enumerate((1, -1)):
+                has = s + 1 < S if way == 1 else s > 0
+                self.start(has, self.own, s, i, way)
+
+        def start(self, has, src, q, slot, way):
+            @pl.when(has)
+            def _():
+                self.copy(src, q, slot, way).start()
+
+            self.open.append((has, src, q, slot, way))
+
+        def step(self, d):
+            for i, way in enumerate((1, -1)):
+                there = s >= d if way == 1 else s + d < S
+                q = lax.rem(s - way * d + S, S)
+
+                @pl.when(there)
+                def _():
+                    self.copy(self.place(q), q, i, way).wait_recv()
+                    if self.hook is not None:
+                        self.hook(q).start()
+
+                on = s + 1 < S if way == 1 else s > 0
+                if d < S - 1:
+                    self.start(jnp.logical_and(there, on), self.place(q), q, 2 * d + i, way)
+
+        def finish(self):
+            for has, src, q, slot, way in self.open:
+                @pl.when(has)
+                def _():
+                    self.copy(src, q, slot, way).wait_send()
+
+    def x_place(q):
+        return xk_all.at[rows(q), xcols(core)]
+
+    def a_place(q):
+        return a_all.at[q, arows(core)]
+
+    def x_twin(q):
+        return remote(x_place(q), x_place(q), sy.at[q], ry.at[q], head=sibling)
+
+    def a_twin(q):
+        return remote(a_place(q), a_place(q), sb.at[q], rb.at[q], head=sibling)
+
+    def x_twin_in(q):
+        there = xk_all.at[rows(q), xcols(1 - core)]
+        return remote(there, there, sy.at[q], ry.at[q], head=sibling)
+
+    def a_twin_in(q):
+        there = a_all.at[q, arows(1 - core)]
+        return remote(there, there, sb.at[q], rb.at[q], head=sibling)
+
+    line_a = Line(a.at[arows(core)], a_place, sa, ra, a_twin)
+    line_x = Line(xk.at[:, xcols(core)], x_place, sx, rx, x_twin)
+    line_x.send()
+    line_a.send()
+    gp, gw = {}, {}
     for k in range(1, S):
-        p = lax.rem(s + k, S)
-        gp[k] = go(remote(pos, pos_all.at[s], sp.at[k], rp.at[k], seq=p))
-        ga[k] = go(remote(a.at[krows(core)], a_all.at[s, krows(core)], sa.at[k], ra.at[k], seq=p))
-        gx[k] = go(remote(xk.at[:, xcols(core)], xk_all.at[rows(s), xcols(core)], sx.at[k], rx.at[k], seq=p))
-    gw = {}
+        gp[k] = go(remote(pos_v, pos_all.at[s], sp.at[k], rp.at[k], seq=lax.rem(s + k, S)))
 
     def wcols(p, c):
         return pl.ds(pl.multiple_of(p * (cw * C) + c * cw, 128), cw)
 
-    for c in range(C):
+    def scatter_w(c):
         for k in range(1, S):
             p = lax.rem(s + k, S)
             gw[c, k] = go(remote(
                 w.at[krows(g), wcols(p, c)], w_all.at[c, s, krows(g)], sw.at[c, k], rw.at[c, k], seq=p))
+
+    scatter_w(0)
     local = []
 
     def fetch(src, dst):
@@ -82,34 +154,13 @@
         local.append(cp)
         return cp
 
-    first = [fetch(w, w_v), fetch(a, a_v), fetch(b, b_v)]
-    own = [fetch(xk, xk_all.at[rows(s)]), fetch(a, a_all.at[s]), fetch(pos, pos_all.at[s])]
+    own = [fetch(b, b_v), fetch(xk, xk_all.at[rows(s)]), fetch(a, a_all.at[s]), fetch(pos_v, pos_all.at[s])]
     own += [fetch(w.at[:, wcols(s, c)], w_all.at[c, s]) for c in range(C)]
-    wts = [fetch(key_up.at[pl.ds(s * hp, hp)], ku_v), fetch(value_up.at[pl.ds(s * hp, hp)], vu_v)]
+    own += [fetch(key_up.at[pl.ds(s * hp, hp)], ku_v), fetch(value_up.at[pl.ds(s * hp, hp)], vu_v)]
     ops = []
     for c in range(C):
         for i in range(S):
             ops.append(fetch(out_proj.at[pl.ds((i * hp + c * heads_c) * vdim, pw)], op_v.at[c, pl.ds(i * pw, pw)]))
-    for cp in first:
-        cp.wait()
-
-    def merge_cols(i, carry):
-        cols = pl.ds(pl.multiple_of(i * cw, 128), cw)
-        m_v[:, cols] = (w_v[:, cols].astype(jnp.float32) + jnp.dot(
-            a_v[...], b_v[:, cols], preferred_element_type=jnp.float32)).astype(jnp.bfloat16)
-        return carry
-
-    lax.fori_loop(0, NC // cw, merge_cols, 0)
-
-    yx, ya = {}, {}
-    for k in range(1, S):
-        q = lax.rem(s - k + S, S)
-        ga[k].wait_recv()
-        ya[k] = go(remote(a_all.at[q, krows(core)], a_all.at[q, krows(core)], sb.at[k], rb.at[k], head=sibling))
-        gx[k].wait_recv()
-        yx[k] = go(remote(xk_all.at[rows(q), xcols(core)], xk_all.at[rows(q), xcols(core)], sy.at[k], ry.at[k], head=sibling))
-    out_m = pltpu.make_async_copy(m_v, merged, loc.at[len(local)])
-    out_m.start()
 
     def forward(c):
         res = {}
@@ -119,13 +170,21 @@
             res[k] = go(remote(w_all.at[c, q, krows(g)], w_all.at[c, q, krows(g)], sv.at[c, k], rv.at[c, k], groups=other))
         return res
 
+    mine = pl.ds(pl.multiple_of(s * pw, 128), pw)
+    lines = []
+    for c in range(C):
+        def h_place(q, c=c):
+            return heads.at[c, :, pl.ds(pl.multiple_of(q * pw, 128), pw)]
+
+        lines.append(Line(h_place(s), h_place, sh.at[c], rh.at[c]))
+
     q_iota = lax.broadcasted_iota(jnp.int32, (S * T, 1), 0)
     k_iota = lax.broadcasted_iota(jnp.int32, (1, S * T), 1)
 
-    def attend(c):
+    def attend(c, between):
         for i in range(S):
-            mm[i * KQ:(i + 1) * KQ] = (w_all[c, i].astype(jnp.float32) + jnp.dot(
-                a_all[i], b_v[:, wcols(s, c)], preferred_element_type=jnp.float32)).astype(jnp.bfloat16)
+            mm[i * KQ:(i + 1) * KQ] = (w_all[c, i].astype(jnp.float32) + lax.dot_general(
+                a_all[i], b_v[:, wcols(s, c)], (((0,), (0,)), ((), ())), preferred_element_type=jnp.float32)).astype(jnp.bfloat16)
         queries = jnp.dot(xk_all[:, :ql], mm[...], preferred_element_type=jnp.float32)
         qpos = q_iota
         kpos = k_iota
@@ -151,55 +210,109 @@
             context = (context / row_sum).astype(jnp.bfloat16)
             res = jnp.dot(context, vu_v[c * heads_c + j], preferred_element_type=jnp.float32).astype(jnp.bfloat16)
             heads[c, :, pl.ds(pl.multiple_of(s * pw + j * vdim, 128), vdim)] = res
-        res = {}
-        mine = pl.ds(pl.multiple_of(s * pw, 128), pw)
-        for k in range(1, S):
-            res[k] = go(remote(heads.at[c, :, mine], heads.at[c, :, mine], sh.at[c, k], rh.at[c, k], seq=lax.rem(s + k, S)))
-        return res
-
-    gh = {}
+            if j == 0:
+                between()
+
+    for d in range(1, S):
+        if d == S - 1:
+            gv = forward(0)
+        line_a.step(d)
+        line_x.step(d)
+        if d == 1:
+            for c in range(1, C):
+                scatter_w(c)
+    for cp in own:
+        cp.wait()
+    for k in range(1, S):
+        q = lax.rem(s + k, S)
+        gp[k].wait_recv()
+        a_twin_in(q).wait_recv()
+        x_twin_in(q).wait_recv()
     for c in range(C):
-        gv = forward(c)
-        if c == 0:
-            for cp in own + wts:
-                cp.wait()
-            for k in range(1, S):
-                gp[k].wait_recv()
-                ya[k].wait_recv()
-                yx[k].wait_recv()
         for k in range(1, S):
             gv[k].wait_recv()
-        gh[c] = attend(c)
+        attend(c, (lambda: None) if c == 0 else (lambda: lines[c - 1].step(1)))
+        if c < C - 1:
+            gv = forward(c + 1)
+        else:
+            lines[c].send()
+        if c > 0:
+            for d in range(2, S):
+                lines[c - 1].step(d)
+        if c < C - 1:
+            lines[c].send()
     for cp in ops:
         cp.wait()
     nb = 2
     bw = dcols // nb
-    go_out = {}
+
+    def trows(i):
+        return pl.ds(pl.multiple_of(i * T, T), T)
+
+    twin, cross = {}, {}
+
+    def reduce_chip(i):
+        for x in range(X):
+            twin[i, x].wait_recv()
+            mid[i, x] = (part[i, trows(2 * x + core)].astype(jnp.float32)
+                         + pair[i, x].astype(jnp.float32)).astype(jnp.bfloat16)
+        for k in range(1, X):
+            x = lax.rem(chip + k, X)
+            cross[i, k] = go(remote(mid.at[i, x], got.at[i, k], so.at[i, k], ro.at[i, k], head=2 * x + core))
+
     for c in range(C):
-        for k in range(1, S):
-            gh[c][k].wait_recv()
         for i in range(nb):
             cols = slice(i * bw, (i + 1) * bw)
+            if c == C - 1 and i == 0:
+                for d in range(2, S):
+                    lines[c].step(d)
             acc = jnp.dot(heads[c], op_v[c, :, cols], preferred_element_type=jnp.float32)
             if c > 0:
                 acc = acc + total[:, cols]
             if c < C - 1:
                 total[:, cols] = acc
+                if c == C - 2 and i == 0:
+                    lines[C - 1].step(1)
             else:
                 part[i] = acc.astype(jnp.bfloat16)
-                for k in range(1, H):
-                    p = lax.rem(h + k, H)
-                    go_out[i, k] = go(remote(
-                        part.at[i, pl.ds(pl.multiple_of(p * T, T), T)], got.at[i, k], so.at[i, k], ro.at[i, k], head=p))
+                for x in range(X):
+                    twin[i, x] = go(remote(
+                        part.at[i, trows(2 * x + 1 - core)], pair.at[i, x], st.at[i, x], rt.at[i, x], head=sibling))
+                if i > 0:
+                    reduce_chip(i - 1)
+    reduce_chip(nb - 1)
     for i in range(nb):
-        res = part[i, pl.ds(pl.multiple_of(h * T, T), T)].astype(jnp.float32)
-        for k in range(1, H):
-            go_out[i, k].wait_recv()
+        res = part[i, trows(h)].astype(jnp.float32) + pair[i, chip].astype(jnp.float32)
+        for k in range(1, X):
+            cross[i, k].wait_recv()
             res = res + got[i, k].astype(jnp.float32)
         mixed[:, i * bw:(i + 1) * bw] = res.astype(jnp.bfloat16)
     for cp in sends:
         cp.wait_send()
-    out_m.wait()
+    for line in [line_x, line_a] + lines:
+        line.finish()
+    for k in range(1, S):
+        q = lax.rem(s + k, S)
+        a_twin(q).wait_send()
+        x_twin(q).wait_send()
+
+
+def merge_kernel(w, a, b, m):
+    m[...] = (w[...].astype(jnp.float32) + lax.dot_general(
+        a[...], b[...], (((0,), (0,)), ((), ())), preferred_element_type=jnp.float32)).astype(jnp.bfloat16)
+
+
+def merge(w, a, b):
+    KQ, NC = w.shape
+    n = NC // 512 if NC % 512 == 0 else 1
+    return pl.pallas_call(
+        merge_kernel,
+        grid=(n,),
+        out_shape=jax.ShapeDtypeStruct(w.shape, w.dtype),
+        in_specs=[pl.BlockSpec((KQ, NC // n), lambda i: (0, i)), pl.BlockSpec(a.shape, lambda i: (0, 0)),
+                  pl.BlockSpec((b.shape[0], NC // n), lambda i: (0, i))],
+        out_specs=pl.BlockSpec((KQ, NC // n), lambda i: (0, i)),
+    )(w, a, b)
 
 
 def fused(mesh_shape, x, kv, positions, w, a, b, key_up, value_up, out_proj):
@@ -217,32 +330,35 @@
     width = ql + kv.shape[1]
     full = -(-width // 256) * 256
     xk = jnp.concatenate([x, kv, jnp.zeros((T, full - width), x.dtype)], axis=1)
-    pos = jnp.broadcast_to(positions[:1].reshape(1, 1), (8, 128))
+    at = jnp.transpose(a)
     scale = 1.0 / math.sqrt(nope + rope)
     dims = (S, H, C, T, KQ, NC, nope, rope, kvr, hp, cw, dcols, scale)
     bf, f32 = jnp.bfloat16, jnp.float32
     dma = pltpu.SemaphoreType.DMA
-    nloc = 3 + 3 + C + 2 + C * S + 1
+    nloc = 4 + C + 2 + C * S
     pw = heads_c * vdim
-    return pl.pallas_call(
+    mixed = pl.pallas_call(
         functools.partial(fused_kernel, dims),
-        out_shape=(jax.ShapeDtypeStruct((KQ, NC), bf), jax.ShapeDtypeStruct((T, dcols), bf)),
-        in_specs=[pl.BlockSpec(memory_space=pl.ANY)] * 8,
-        out_specs=(pl.BlockSpec(memory_space=pl.ANY), pl.BlockSpec(memory_space=pltpu.VMEM)),
+        out_shape=jax.ShapeDtypeStruct((T, dcols), bf),
+        in_specs=[pl.BlockSpec(memory_space=pltpu.SMEM)] + [pl.BlockSpec(memory_space=pl.ANY)] * 7,
+        out_specs=pl.BlockSpec(memory_space=pltpu.VMEM),
         scratch_shapes=[
-            pltpu.VMEM((KQ, NC), bf), pltpu.VMEM(a.shape, bf), pltpu.VMEM(b.shape, bf), pltpu.VMEM((KQ, NC), bf),
-            pltpu.VMEM((S * T, full), bf), pltpu.VMEM((S,) + a.shape, bf), pltpu.VMEM((S, 8, 128), jnp.int32),
+            pltpu.VMEM(b.shape, bf), pltpu.VMEM((8, 128), jnp.int32),
+            pltpu.VMEM((S * T, full), bf), pltpu.VMEM((S,) + at.shape, bf), pltpu.VMEM((S, 8, 128), jnp.int32),
             pltpu.VMEM((C, S, KQ, cw), bf), pltpu.VMEM((S * KQ, cw), bf),
             pltpu.VMEM((hp, nope, kvr), bf), pltpu.VMEM((hp, kvr, vdim), bf),
             pltpu.VMEM((C, S * pw, dcols), bf), pltpu.VMEM((C, S * T, S * pw), bf), pltpu.VMEM((S * T, dcols), f32),
-            pltpu.VMEM((2, S * T, dcols // 2), bf), pltpu.VMEM((2, H, T, dcols // 2), bf),
+            pltpu.VMEM((2, S * T, dcols // 2), bf), pltpu.VMEM((2, H // 2, T, dcols // 2), bf),
+            pltpu.VMEM((2, H // 2, T, dcols // 2), bf), pltpu.VMEM((2, H // 2, T, dcols // 2), bf),
             dma((nloc,)),
-            dma((S,)), dma((S,)), dma((S,)), dma((S,)), dma((S,)), dma((S,)), dma((S,)), dma((S,)), dma((S,)), dma((S,)),
-            dma((C, S)), dma((C, S)), dma((C, S)), dma((C, S)), dma((C, S)), dma((C, S)),
-            dma((2, H)), dma((2, H)),
+            dma((2 * S,)), dma((S,)), dma((S,)), dma((S,)), dma((2 * S,)), dma((S,)), dma((S,)), dma((S,)),
+            dma((S,)), dma((S,)),
+            dma((C, S)), dma((C, S)), dma((C, S)), dma((C, S)), dma((C, 2 * S)), dma((C, S)),
+            dma((2, H // 2)), dma((2, H // 2)), dma((2, H // 2)), dma((2, H // 2)),
         ],
         compiler_params=pltpu.CompilerParams(collective_id=0, has_side_effects=True),
-    )(w, xk, a, pos, b, key_up, value_up, out_proj)
+    )(positions, w, xk, at, b, key_up, value_up, out_proj)
+    return merge(w, at, b), mixed
 
 
 def fits(shape, x, kv, w, a, key_up, value_up, out_proj):
@@ -250,8 +366,8 @@
     hd, nope, kvr = key_up.shape
     rope = kv.shape[1] - kvr
     return (
-        shape["groups"] == 2 and S > 1 and H == S and H % 2 == 0 and hd % (2 * S) == 0
-        and (2 * (nope + rope)) % 128 == 0 and w.shape[0] % 32 == 0 and x.shape[0] % 16 == 0
+        shape["groups"] == 2 and S > 1 and H == S and H % 2 == 0 and hd % (4 * S) == 0
+        and (2 * (nope + rope)) % 128 == 0 and w.shape[0] % 32 == 0 and a.shape[1] % 32 == 0 and x.shape[0] % 16 == 0
         and nope % 128 == 0 and kvr % 128 == 0 and value_up.shape[2] % 128 == 0
         and x.shape[1] % 128 == 0 and out_proj.shape[1] % 256 == 0
     )

time: 103 us -> 99.4 us (0.965)
  the two profiles are of different devices: /device:TPU:25 before, /device:TPU:0 now
where the time goes in v2:
time: 99.4 us; the launch traced here: 99.1 us
  Pallas kernels  95.9 us (96%)
  local copies, waits for them, and re-layouts  2.57 us (3%)
    pallas_call x1, Pallas kernels, fused(): pl.pallas_call(functools.partial(fused_kernel, dims), out_shape=jax.Shape...  90.3 us
    pallas_call x1, Pallas kernels, merge(): pl.pallas_call(merge_kernel, grid=(n,), out_shape=jax.ShapeDtypeStruct(w....  5.62 us

profile of v2, /device:TPU:0, one launch (start us, length us, event | category | flops | bytes accessed | tf_op | source)
XLA Modules:
  0.0 99.1 jit_solution(14363815100161887861)
XLA Ops:
  0.6 1.8 %concatenate.3.xk = bf16[80,2304]{1,0:T(8,128)(2,1)} concatenate(bf16[80,1536]{1,0:T(8,128)(2,1)} %param.9, bf16[80,576]{1,0:T(8,128)(2,1)} %param.10, bf16[80,192]{1,0:T(8,128)(2,1)S(1)} %broadcast_in_dim.3), dimensions={1} | concatenate | bytes 737280 | tf_op jit(solution)/shard_map/concatenate | solution.py:332
  2.5 90.3 %shard_map.105 = bf16[80,1792]{1,0:T(8,128)(2,1)} custom-call(s32[80]{0:T(128)} %pos.1, bf16[384,3072]{1,0:T(8,128)(2,1)} %w.3, bf16[80,2304]{1,0:T(8,128)(2,1)} %concatenate.3.xk, bf16[64,384]{1,0:T(8,128)(2,1)} %bitcast.1, bf16[64,3072]{1,0:T(8,128)(2,1)} %b.3, bf16[16,128,512]{2,1,0:T(8,128)(2,1)} %key_up.1, bf16[16,512,128]{2,1,0:T(8,128)(2,1)} %value_up.1, ...), custom_call_target="tpu_custom_call" | custom-call | tf_op jit(solution)/shard_map/pallas_call | solution.py:340
  92.8 0.0 copy-start
  92.8 5.6 %shard_map.104 = bf16[384,3072]{1,0:T(8,128)(2,1)} custom-call(bf16[384,3072]{1,0:T(8,128)(2,1)} %w.3, bf16[64,384]{1,0:T(8,128)(2,1)} %bitcast.2, bf16[64,3072]{1,0:T(8,128)(2,1)} %b.3), custom_call_target="tpu_custom_call" | custom-call | tf_op jit(solution)/shard_map/pallas_call | solution.py:308
  98.4 0.0 copy-done
  98.4 0.7 copy.12
  (1 shorter events, 0.0 us)
Async XLA Ops:
  92.8 5.6 %copy-start = (bf16[80,1792]{1,0:T(8,128)(2,1)S(1)}, bf16[80,1792]{1,0:T(8,128)(2,1)}, u32[]{:S(2)}) copy-start(bf16[80,1792]{1,0:T(8,128)(2,1)} %shard_map.105) | copy-start | bytes 860164

commit v3 on v2

--- a/solution.py
+++ b/solution.py
@@ -12,14 +12,14 @@
 MESH = pl.DeviceIdType.MESH
 
 
-def fused_kernel(dims, pos, w, xk, a, b, key_up, value_up, out_proj, mixed,
-                 b_v, pos_v, xk_all, a_all, pos_all, w_all, mm, ku_v, vu_v, op_v, heads, total,
+def fused_kernel(dims, pos, w, xk, a, b, key_up, value_up, out_proj, merged, mixed,
+                 w_v, m_v, b_v, pos_v, xk_all, a_all, pos_all, w_all, mm, ku_v, vu_v, op_v, heads, total,
                  part, pair, mid, got, loc, sx, rx, sy, ry, sa, ra, sb, rb, sp, rp, sw, rw, sv, rv, sh, rh,
                  st, rt, so, ro):
     S, H, C, T, KQ, NC, nope, rope, kvr, hp, cw, dcols, scale = dims
     qw = nope + rope
     half_k = KQ // 2
-    half_x = xk.shape[1] // 2
+    part_x = xk.shape[1] // H
     ql = S * KQ
     pw = (cw // qw) * (out_proj.shape[0] // (hp * S))
     heads_c = cw // qw
@@ -30,7 +30,7 @@
     other = 1 - g
     pos_v[...] = jnp.full(pos_v.shape, pos[0], jnp.int32)
     core = lax.rem(h, 2)
-    half_a = a.shape[0] // 2
+    part_a = a.shape[0] // H
     X = H // 2
     chip = h // 2
     sibling = h + 1 - 2 * core
@@ -58,13 +58,13 @@
         return pl.ds(pl.multiple_of(i * T, T), T)
 
     def xcols(i):
-        return pl.ds(pl.multiple_of(i * half_x, 128), half_x)
+        return pl.ds(pl.multiple_of(i * part_x, 128), part_x)
 
     def krows(i):
         return pl.ds(pl.multiple_of(i * half_k, 16), half_k)
 
     def arows(i):
-        return pl.ds(pl.multiple_of(i * half_a, 16), half_a)
+        return pl.ds(pl.multiple_of(i * part_a, 16), part_a)
 
     class Line:
         def __init__(self, own, place, ss, rs, hook=None):
@@ -108,33 +108,12 @@
                 def _():
                     self.copy(src, q, slot, way).wait_send()
 
-    def x_place(q):
-        return xk_all.at[rows(q), xcols(core)]
-
-    def a_place(q):
-        return a_all.at[q, arows(core)]
-
-    def x_twin(q):
-        return remote(x_place(q), x_place(q), sy.at[q], ry.at[q], head=sibling)
-
-    def a_twin(q):
-        return remote(a_place(q), a_place(q), sb.at[q], rb.at[q], head=sibling)
-
-    def x_twin_in(q):
-        there = xk_all.at[rows(q), xcols(1 - core)]
-        return remote(there, there, sy.at[q], ry.at[q], head=sibling)
-
-    def a_twin_in(q):
-        there = a_all.at[q, arows(1 - core)]
-        return remote(there, there, sb.at[q], rb.at[q], head=sibling)
-
-    line_a = Line(a.at[arows(core)], a_place, sa, ra, a_twin)
-    line_x = Line(xk.at[:, xcols(core)], x_place, sx, rx, x_twin)
-    line_x.send()
-    line_a.send()
-    gp, gw = {}, {}
+    gp, gw, gx, ga, yx, ya = {}, {}, {}, {}, {}, {}
     for k in range(1, S):
-        gp[k] = go(remote(pos_v, pos_all.at[s], sp.at[k], rp.at[k], seq=lax.rem(s + k, S)))
+        p = lax.rem(s + k, S)
+        gx[k] = go(remote(xk.at[:, xcols(h)], xk_all.at[rows(s), xcols(h)], sx.at[k], rx.at[k], seq=p))
+        ga[k] = go(remote(a.at[arows(h)], a_all.at[s, arows(h)], sa.at[k], ra.at[k], seq=p))
+        gp[k] = go(remote(pos_v, pos_all.at[s], sp.at[k], rp.at[k], seq=p))
 
     def wcols(p, c):
         return pl.ds(pl.multiple_of(p * (cw * C) + c * cw, 128), cw)
@@ -145,7 +124,8 @@
             gw[c, k] = go(remote(
                 w.at[krows(g), wcols(p, c)], w_all.at[c, s, krows(g)], sw.at[c, k], rw.at[c, k], seq=p))
 
-    scatter_w(0)
+    for c in range(C):
+        scatter_w(c)
     local = []
 
     def fetch(src, dst):
@@ -154,7 +134,7 @@
         local.append(cp)
         return cp
 
-    own = [fetch(b, b_v), fetch(xk, xk_all.at[rows(s)]), fetch(a, a_all.at[s]), fetch(pos_v, pos_all.at[s])]
+    own = [fetch(b, b_v), fetch(w, w_v), fetch(a, a_all.at[s]), fetch(xk, xk_all.at[rows(s)]), fetch(pos_v, pos_all.at[s])]
     own += [fetch(w.at[:, wcols(s, c)], w_all.at[c, s]) for c in range(C)]
     own += [fetch(key_up.at[pl.ds(s * hp, hp)], ku_v), fetch(value_up.at[pl.ds(s * hp, hp)], vu_v)]
     ops = []
@@ -213,21 +193,36 @@
             if j == 0:
                 between()
 
-    for d in range(1, S):
-        if d == S - 1:
-            gv = forward(0)
-        line_a.step(d)
-        line_x.step(d)
-        if d == 1:
-            for c in range(1, C):
-                scatter_w(c)
+    for k in range(1, S):
+        q = lax.rem(s - k + S, S)
+        gx[k].wait_recv()
+        for j in range(1, H):
+            to = lax.rem(h + j, H)
+            yx[k, j] = go(remote(
+                xk_all.at[rows(q), xcols(h)], xk_all.at[rows(q), xcols(h)], sy.at[k, j], ry.at[k, j], head=to))
+        ga[k].wait_recv()
+        for j in range(1, H):
+            to = lax.rem(h + j, H)
+            ya[k, j] = go(remote(
+                a_all.at[q, arows(h)], a_all.at[q, arows(h)], sb.at[k, j], rb.at[k, j], head=to))
     for cp in own:
         cp.wait()
+
+    def merge_cols(i, carry):
+        cols = pl.ds(pl.multiple_of(i * cw, 128), cw)
+        m_v[:, cols] = (w_v[:, cols].astype(jnp.float32) + lax.dot_general(
+            a_all[s], b_v[:, cols], (((0,), (0,)), ((), ())), preferred_element_type=jnp.float32)).astype(jnp.bfloat16)
+        return carry
+
+    lax.fori_loop(0, NC // cw, merge_cols, 0)
+    out_m = pltpu.make_async_copy(m_v, merged, loc.at[len(local)])
+    out_m.start()
+    gv = forward(0)
     for k in range(1, S):
-        q = lax.rem(s + k, S)
         gp[k].wait_recv()
-        a_twin_in(q).wait_recv()
-        x_twin_in(q).wait_recv()
+        for j in range(1, H):
+            ya[k, j].wait_recv()
+            yx[k, j].wait_recv()
     for c in range(C):
         for k in range(1, S):
             gv[k].wait_recv()
@@ -289,30 +284,9 @@
         mixed[:, i * bw:(i + 1) * bw] = res.astype(jnp.bfloat16)
     for cp in sends:
         cp.wait_send()
-    for line in [line_x, line_a] + lines:
+    for line in lines:
         line.finish()
-    for k in range(1, S):
-        q = lax.rem(s + k, S)
-        a_twin(q).wait_send()
-        x_twin(q).wait_send()
-
-
-def merge_kernel(w, a, b, m):
-    m[...] = (w[...].astype(jnp.float32) + lax.dot_general(
-        a[...], b[...], (((0,), (0,)), ((), ())), preferred_element_type=jnp.float32)).astype(jnp.bfloat16)
-
-
-def merge(w, a, b):
-    KQ, NC = w.shape
-    n = NC // 512 if NC % 512 == 0 else 1
-    return pl.pallas_call(
-        merge_kernel,
-        grid=(n,),
-        out_shape=jax.ShapeDtypeStruct(w.shape, w.dtype),
-        in_specs=[pl.BlockSpec((KQ, NC // n), lambda i: (0, i)), pl.BlockSpec(a.shape, lambda i: (0, 0)),
-                  pl.BlockSpec((b.shape[0], NC // n), lambda i: (0, i))],
-        out_specs=pl.BlockSpec((KQ, NC // n), lambda i: (0, i)),
-    )(w, a, b)
+    out_m.wait()
 
 
 def fused(mesh_shape, x, kv, positions, w, a, b, key_up, value_up, out_proj):
@@ -328,21 +302,22 @@
     cw = heads_c * (nope + rope)
     dcols = out_proj.shape[1]
     width = ql + kv.shape[1]
-    full = -(-width // 256) * 256
+    full = -(-width // (128 * H)) * (128 * H)
     xk = jnp.concatenate([x, kv, jnp.zeros((T, full - width), x.dtype)], axis=1)
     at = jnp.transpose(a)
     scale = 1.0 / math.sqrt(nope + rope)
     dims = (S, H, C, T, KQ, NC, nope, rope, kvr, hp, cw, dcols, scale)
     bf, f32 = jnp.bfloat16, jnp.float32
     dma = pltpu.SemaphoreType.DMA
-    nloc = 4 + C + 2 + C * S
+    nloc = 5 + C + 2 + C * S + 1
     pw = heads_c * vdim
-    mixed = pl.pallas_call(
+    return pl.pallas_call(
         functools.partial(fused_kernel, dims),
-        out_shape=jax.ShapeDtypeStruct((T, dcols), bf),
+        out_shape=(jax.ShapeDtypeStruct((KQ, NC), bf), jax.ShapeDtypeStruct((T, dcols), bf)),
         in_specs=[pl.BlockSpec(memory_space=pltpu.SMEM)] + [pl.BlockSpec(memory_space=pl.ANY)] * 7,
-        out_specs=pl.BlockSpec(memory_space=pltpu.VMEM),
+        out_specs=(pl.BlockSpec(memory_space=pl.ANY), pl.BlockSpec(memory_space=pltpu.VMEM)),
         scratch_shapes=[
+            pltpu.VMEM((KQ, NC), bf), pltpu.VMEM((KQ, NC), bf),
             pltpu.VMEM(b.shape, bf), pltpu.VMEM((8, 128), jnp.int32),
             pltpu.VMEM((S * T, full), bf), pltpu.VMEM((S,) + at.shape, bf), pltpu.VMEM((S, 8, 128), jnp.int32),
             pltpu.VMEM((C, S, KQ, cw), bf), pltpu.VMEM((S * KQ, cw), bf),
@@ -351,14 +326,13 @@
             pltpu.VMEM((2, S * T, dcols // 2), bf), pltpu.VMEM((2, H // 2, T, dcols // 2), bf),
             pltpu.VMEM((2, H // 2, T, dcols // 2), bf), pltpu.VMEM((2, H // 2, T, dcols // 2), bf),
             dma((nloc,)),
-            dma((2 * S,)), dma((S,)), dma((S,)), dma((S,)), dma((2 * S,)), dma((S,)), dma((S,)), dma((S,)),
+            dma((S,)), dma((S,)), dma((S, H)), dma((S, H)), dma((S,)), dma((S,)), dma((S, H)), dma((S, H)),
             dma((S,)), dma((S,)),
             dma((C, S)), dma((C, S)), dma((C, S)), dma((C, S)), dma((C, 2 * S)), dma((C, S)),
             dma((2, H // 2)), dma((2, H // 2)), dma((2, H // 2)), dma((2, H // 2)),
         ],
         compiler_params=pltpu.CompilerParams(collective_id=0, has_side_effects=True),
     )(positions, w, xk, at, b, key_up, value_up, out_proj)
-    return merge(w, at, b), mixed
 
 
 def fits(shape, x, kv, w, a, key_up, value_up, out_proj):
@@ -367,7 +341,7 @@
     rope = kv.shape[1] - kvr
     return (
         shape["groups"] == 2 and S > 1 and H == S and H % 2 == 0 and hd % (4 * S) == 0
-        and (2 * (nope + rope)) % 128 == 0 and w.shape[0] % 32 == 0 and a.shape[1] % 32 == 0 and x.shape[0] % 16 == 0
+        and (2 * (nope + rope)) % 128 == 0 and w.shape[0] % 32 == 0 and a.shape[1] % (16 * H) == 0 and x.shape[0] % 16 == 0
         and nope % 128 == 0 and kvr % 128 == 0 and value_up.shape[2] % 128 == 0
         and x.shape[1] % 128 == 0 and out_proj.shape[1] % 256 == 0
     )

time: 99.4 us -> 91.3 us (0.919)
  Pallas kernels: 95.9 us -> 84.6 us
  local copies, waits for them, and re-layouts: 2.57 us -> 5.87 us
    pallas_call x2 -> x1, Pallas kernels: 95.9 us -> 84.6 us  [fused(): pl.pallas_call(functools.partial(fused_kernel, dims), out_shape=(jax.Shap...]
    unnamed x3 -> x4, local copies, waits for them, and re-layouts: 0.72 us -> 3.98 us
where the time goes in v3:
time: 91.3 us; the launch traced here: 91.1 us
  Pallas kernels  84.6 us (93%)
  local copies, waits for them, and re-layouts  5.87 us (6%)
    pallas_call x1, Pallas kernels, fused(): pl.pallas_call(functools.partial(fused_kernel, dims), out_shape=(jax.Shap...  84.6 us
    unnamed x4, local copies, waits for them, and re-layouts  3.98 us
    concatenate x1, local copies, waits for them, and re-layouts, fused(): xk = jnp.concatenate([x, kv, jnp.zeros((T, full - width), x.dtype)], axis=1)  1.88 us

profile of v3, /device:TPU:0, one launch (start us, length us, event | category | flops | bytes accessed | tf_op | source)
XLA Modules:
  0.0 91.1 jit_solution(13158198989924661114)
XLA Ops:
  0.6 1.9 %concatenate.3.xk = bf16[80,2560]{1,0:T(8,128)(2,1)} concatenate(bf16[80,1536]{1,0:T(8,128)(2,1)} %param.9, bf16[80,576]{1,0:T(8,128)(2,1)} %param.10, bf16[80,448]{1,0:T(8,128)(2,1)S(1)} %broadcast_in_dim.3), dimensions={1} | concatenate | bytes 819200 | tf_op jit(solution)/shard_map/concatenate | solution.py:306
  2.5 84.6 %shard_map.104 = (bf16[384,3072]{1,0:T(8,128)(2,1)}, bf16[80,1792]{1,0:T(8,128)(2,1)}) custom-call(s32[80]{0:T(128)} %pos.1, bf16[384,3072]{1,0:T(8,128)(2,1)} %w.1, bf16[80,2560]{1,0:T(8,128)(2,1)} %concatenate.3.xk, bf16[64,384]{1,0:T(8,128)(2,1)} %bitcast.1, bf16[64,3072]{1,0:T(8,128)(2,1)} %b.1, bf16[16,128,512]{2,1,0:T(8,128)(2,1)} %key_up.1, ...), custom_call_target="tpu_custom_call" | custom-call | tf_op jit(solution)/shard_map/pallas_call | solution.py:314
  87.1 0.0 copy-start
  87.1 3.3 %copy.13 = bf16[384,3072]{1,0:T(8,128)(2,1)} copy(bf16[384,3072]{1,0:T(8,128)(2,1)} %get-tuple-element.4) | data formatting | bytes 4718592
  90.4 0.0 copy-done
  90.4 0.7 copy.14
  (1 shorter events, 0.0 us)
Async XLA Ops:
  87.1 3.3 %copy-start = (bf16[80,1792]{1,0:T(8,128)(2,1)S(1)}, bf16[80,1792]{1,0:T(8,128)(2,1)}, u32[]{:S(2)}) copy-start(bf16[80,1792]{1,0:T(8,128)(2,1)} %get-tuple-element.5) | copy-start | bytes 860164

commit v4 on v3

--- a/solution.py
+++ b/solution.py
@@ -226,9 +226,17 @@
     for c in range(C):
         for k in range(1, S):
             gv[k].wait_recv()
-        attend(c, (lambda: None) if c == 0 else (lambda: lines[c - 1].step(1)))
+        later = []
+
+        def between():
+            if c > 0:
+                lines[c - 1].step(1)
+            if c < C - 1:
+                later.append(forward(c + 1))
+
+        attend(c, between)
         if c < C - 1:
-            gv = forward(c + 1)
+            gv = later[0]
         else:
             lines[c].send()
         if c > 0:

time: 91.3 us -> 90.5 us (level)
  no operation moved by 1% of the time
where the time goes in v4:
time: 90.5 us; the launch traced here: 90.3 us
  Pallas kernels  83.8 us (93%)
  local copies, waits for them, and re-layouts  5.87 us (6%)
    pallas_call x1, Pallas kernels, fused(): pl.pallas_call(functools.partial(fused_kernel, dims), out_shape=(jax.Shap...  83.8 us
    unnamed x4, local copies, waits for them, and re-layouts  3.98 us
    concatenate x1, local copies, waits for them, and re-layouts, fused(): xk = jnp.concatenate([x, kv, jnp.zeros((T, full - width), x.dtype)], axis=1)  1.88 us

profile of v4, /device:TPU:0, one launch (start us, length us, event | category | flops | bytes accessed | tf_op | source)
XLA Modules:
  0.0 90.3 jit_solution(6415072866534202233)
XLA Ops:
  0.6 1.9 %concatenate.3.xk = bf16[80,2560]{1,0:T(8,128)(2,1)} concatenate(bf16[80,1536]{1,0:T(8,128)(2,1)} %param.9, bf16[80,576]{1,0:T(8,128)(2,1)} %param.10, bf16[80,448]{1,0:T(8,128)(2,1)S(1)} %broadcast_in_dim.3), dimensions={1} | concatenate | bytes 819200 | tf_op jit(solution)/shard_map/concatenate | solution.py:314
  2.5 83.8 %shard_map.104 = (bf16[384,3072]{1,0:T(8,128)(2,1)}, bf16[80,1792]{1,0:T(8,128)(2,1)}) custom-call(s32[80]{0:T(128)} %pos.1, bf16[384,3072]{1,0:T(8,128)(2,1)} %w.1, bf16[80,2560]{1,0:T(8,128)(2,1)} %concatenate.3.xk, bf16[64,384]{1,0:T(8,128)(2,1)} %bitcast.1, bf16[64,3072]{1,0:T(8,128)(2,1)} %b.1, bf16[16,128,512]{2,1,0:T(8,128)(2,1)} %key_up.1, ...), custom_call_target="tpu_custom_call" | custom-call | tf_op jit(solution)/shard_map/pallas_call | solution.py:322
  86.3 0.0 copy-start
  86.3 3.3 %copy.13 = bf16[384,3072]{1,0:T(8,128)(2,1)} copy(bf16[384,3072]{1,0:T(8,128)(2,1)} %get-tuple-element.4) | data formatting | bytes 4718592
  89.6 0.0 copy-done
  89.6 0.7 copy.14
  (1 shorter events, 0.0 us)
Async XLA Ops:
  86.3 3.3 %copy-start = (bf16[80,1792]{1,0:T(8,128)(2,1)S(1)}, bf16[80,1792]{1,0:T(8,128)(2,1)}, u32[]{:S(2)}) copy-start(bf16[80,1792]{1,0:T(8,128)(2,1)} %get-tuple-element.5) | copy-start | bytes 860164
